TPU v7x, 128 devices: a whole 4x4x4 slice. The times are simulated.
128 devices in a mesh: wide: 16 (over x, z), narrow: 8 (over y, core).
Axes of the slice: x: 4, y: 4, z: 4, core: 2. Of those that a mesh axis runs over, the one named last changes fastest.
Arguments:
- tensor_slab: float32 [512, 512, 2048], P(None, 'wide', 'narrow'), may hold values from -220 to 220
- start_basis: float32 [512, 64], replicated, may hold values from -6 to 6
Outputs:
- factor_basis: float32 [512, 64], replicated
- core_unfold: float32 [2048, 64, 512], P('narrow', 'wide')
All inputs are finite; a program needn't handle non-finite values.
Results may differ from a plain program's by a relative error of at most 0.0003.
Values sent between devices are 32-bit elements; how exact they have to be, the bound alone decides.
A program may use at most 64 MiB of HBM per device.

v0:
```python
import jax
import jax.numpy as jnp
from jax import lax
from jax.sharding import PartitionSpec as P

I1 = 512
ITERS = 8


def orthonormal(block, inner):
    lower_factor = jnp.linalg.cholesky(inner)
    return jax.scipy.linalg.solve_triangular(lower_factor, block.T, lower=True).T


def shards(tensor_slab, start_basis):
    highest = lax.Precision.HIGHEST
    unfold = tensor_slab.reshape(I1, -1)
    basis = start_basis
    local_gram = jnp.dot(unfold, unfold.T, precision=highest, preferred_element_type=jnp.float32)
    gram_full = lax.psum(local_gram, ("wide", "narrow"))
    for sweep_index in range(ITERS):
        block = jnp.dot(gram_full, basis, precision=highest)
        basis = orthonormal(block, jnp.dot(block.T, block, precision=highest))
    core_local = jnp.einsum("ir,ijl->lrj", basis, tensor_slab, precision=highest)
    core_unfold = lax.all_to_all(core_local, "wide", split_axis=1, concat_axis=2, tiled=True)
    return (basis, core_unfold)


def solution(mesh):
    placed = (P(None, "wide", "narrow"), P())
    return jax.shard_map(
        shards,
        mesh=mesh,
        in_specs=placed,
        out_specs=(P(), P("narrow", "wide", None)),
        check_vma=False,
    )
```

profile of v0, /device:TPU:1, one launch (start us, length us, event | category | flops | bytes accessed | tf_op | source)
XLA Modules:
  0.0 389.1 jit_solution(11629814040123961032)
XLA Ops:
  7.2 40.1 %fusion.7 = f32[512,512]{1,0:T(8,128)} fusion(f32[512,32,256]{2,1,0:T(8,128)} %param.5), kind=kOutput, calls=%fused_computation.5 | convolution fusion | flops 25769803776 | bytes 17825792 | tf_op jit(solution)/shard_map/dot_general | solution.py:19
  47.3 150.7 %all-reduce.2.cloned.1.call-done = f32[512,512]{1,0:T(8,128)} async-done(((f32[512,512]{1,0:T(8,128)}), f32[512,512]{1,0:T(8,128)}) %all-reduce.2.cloned.1.call-update) | async-done | bytes 1048592 | tf_op jit(solution)/shard_map/psum | solution.py:20
  198.0 2.4 fusion.65
  200.7 5.8 %cholesky.134 = f32[64,64]{1,0:T(8,128)S(1)} custom-call(f32[64,64]{1,0:T(8,128)S(1)} %fusion.50), custom_call_target="Cholesky" | custom-call | tf_op jit(solution)/shard_map/jit(cholesky)/cholesky | solution.py:11
  207.3 0.7 fusion.27
  207.9 4.9 %custom-call.12 = f32[1,64,64]{1,2,0:T(8,128)S(1)} custom-call(f32[1,64,64]{2,1,0:T(8,128)S(1)} %fusion.27), custom_call_target="InvertDiagBlocksLowerTriangular" | custom-call | tf_op jit(solution)/shard_map/jit(_solve_triangular)/triangular_solve | solution.py:12
  213.2 2.4 fusion.67
  215.9 5.8 %cholesky.145 = f32[64,64]{1,0:T(8,128)S(1)} custom-call(f32[64,64]{1,0:T(8,128)S(1)} %fusion.48), custom_call_target="Cholesky" | custom-call | tf_op jit(solution)/shard_map/jit(cholesky)/cholesky | solution.py:11
  222.4 0.7 fusion.28
  223.1 4.9 %custom-call.13 = f32[1,64,64]{1,2,0:T(8,128)S(1)} custom-call(f32[1,64,64]{2,1,0:T(8,128)S(1)} %fusion.28), custom_call_target="InvertDiagBlocksLowerTriangular" | custom-call | tf_op jit(solution)/shard_map/jit(_solve_triangular)/triangular_solve | solution.py:12
  228.3 2.4 fusion.69
  231.0 5.8 %cholesky.156 = f32[64,64]{1,0:T(8,128)S(1)} custom-call(f32[64,64]{1,0:T(8,128)S(1)} %fusion.46), custom_call_target="Cholesky" | custom-call | tf_op jit(solution)/shard_map/jit(cholesky)/cholesky | solution.py:11
  238.2 4.9 %custom-call.14 = f32[1,64,64]{1,2,0:T(8,128)S(1)} custom-call(f32[1,64,64]{2,1,0:T(8,128)S(1)} %fusion.29), custom_call_target="InvertDiagBlocksLowerTriangular" | custom-call | tf_op jit(solution)/shard_map/jit(_solve_triangular)/triangular_solve | solution.py:12
  243.5 2.4 fusion.71
  246.2 5.8 %cholesky.167 = f32[64,64]{1,0:T(8,128)S(1)} custom-call(f32[64,64]{1,0:T(8,128)S(1)} %fusion.44), custom_call_target="Cholesky" | custom-call | tf_op jit(solution)/shard_map/jit(cholesky)/cholesky | solution.py:11
  253.4 4.9 %custom-call.15 = f32[1,64,64]{1,2,0:T(8,128)S(1)} custom-call(f32[1,64,64]{2,1,0:T(8,128)S(1)} %fusion.30), custom_call_target="InvertDiagBlocksLowerTriangular" | custom-call | tf_op jit(solution)/shard_map/jit(_solve_triangular)/triangular_solve | solution.py:12
  258.6 2.5 fusion.73
  261.5 5.8 %cholesky.178 = f32[64,64]{1,0:T(8,128)S(1)} custom-call(f32[64,64]{1,0:T(8,128)S(1)} %fusion.42), custom_call_target="Cholesky" | custom-call | tf_op jit(solution)/shard_map/jit(cholesky)/cholesky | solution.py:11
  268.7 4.9 %custom-call.16 = f32[1,64,64]{1,2,0:T(8,128)S(1)} custom-call(f32[1,64,64]{2,1,0:T(8,128)S(1)} %fusion.31), custom_call_target="InvertDiagBlocksLowerTriangular" | custom-call | tf_op jit(solution)/shard_map/jit(_solve_triangular)/triangular_solve | solution.py:12
  273.9 2.4 fusion.75
  276.6 5.8 %cholesky.189 = f32[64,64]{1,0:T(8,128)S(1)} custom-call(f32[64,64]{1,0:T(8,128)S(1)} %fusion.40), custom_call_target="Cholesky" | custom-call | tf_op jit(solution)/shard_map/jit(cholesky)/cholesky | solution.py:11
  283.8 4.9 %custom-call.17 = f32[1,64,64]{1,2,0:T(8,128)S(1)} custom-call(f32[1,64,64]{2,1,0:T(8,128)S(1)} %fusion.32), custom_call_target="InvertDiagBlocksLowerTriangular" | custom-call | tf_op jit(solution)/shard_map/jit(_solve_triangular)/triangular_solve | solution.py:12
  289.1 2.4 fusion.77
  291.8 5.8 %cholesky.200 = f32[64,64]{1,0:T(8,128)S(1)} custom-call(f32[64,64]{1,0:T(8,128)S(1)} %fusion.38), custom_call_target="Cholesky" | custom-call | tf_op jit(solution)/shard_map/jit(cholesky)/cholesky | solution.py:11
  299.0 4.9 %custom-call.18 = f32[1,64,64]{1,2,0:T(8,128)S(1)} custom-call(f32[1,64,64]{2,1,0:T(8,128)S(1)} %fusion.33), custom_call_target="InvertDiagBlocksLowerTriangular" | custom-call | tf_op jit(solution)/shard_map/jit(_solve_triangular)/triangular_solve | solution.py:12
  304.2 2.4 fusion.79
  306.9 5.8 %cholesky.211 = f32[64,64]{1,0:T(8,128)S(1)} custom-call(f32[64,64]{1,0:T(8,128)S(1)} %fusion.36), custom_call_target="Cholesky" | custom-call | tf_op jit(solution)/shard_map/jit(cholesky)/cholesky | solution.py:11
  314.1 4.9 %custom-call.19 = f32[1,64,64]{1,2,0:T(8,128)S(1)} custom-call(f32[1,64,64]{2,1,0:T(8,128)S(1)} %fusion.34), custom_call_target="InvertDiagBlocksLowerTriangular" | custom-call | tf_op jit(solution)/shard_map/jit(_solve_triangular)/triangular_solve | solution.py:12
  319.4 25.8 %fusion.4 = f32[256,64,32]{0,1,2:T(8,128)S(1)} fusion(f32[512,32,256]{2,1,0:T(8,128)} %param.5, f32[64,512]{1,0:T(8,128)S(1)} %fusion.11), kind=kOutput, calls=%fused_computation.4 | convolution fusion | flops 3221225472 | bytes 19005440 | tf_op jit(solution)/shard_map/ir,ijl->lrj/dot_general | solution.py:24
  345.2 1.2 copy.53
  346.4 33.5 %all_to_all.18 = f32[256,64,32]{0,2,1:T(8,128)S(1)} all-to-all(f32[256,64,32]{0,2,1:T(8,128)S(1)} %copy.53), channel_id=1, replica_groups=mesh['wide'=16,'narrow'=8] {'wide'}, dimensions={1} | all-to-all | bytes 4194304 | tf_op jit(solution)/shard_map/all_to_all | solution.py:25
  380.1 2.0 copy.55
  (61 shorter events, 15.0 us)
Async XLA Ops:
  7.2 190.9 %copy-start = (f32[512,64]{0,1:T(8,128)S(1)}, f32[512,64]{0,1:T(8,128)}, u32[]{:S(2)}) copy-start(f32[512,64]{0,1:T(8,128)} %param.6) | copy-start | bytes 393220
  7.2 190.9 %all-reduce.2.cloned.1.call-start = ((), (), s32[]{:S(2)}) async-start(), calls=%async_computation.1 | async-start | bytes 2097152 | tf_op jit(solution)/shard_map/psum | solution.py:20
  319.4 62.7 %copy-start.1 = (f32[64,512]{1,0:T(8,128)}, f32[64,512]{1,0:T(8,128)S(1)}, u32[]{:S(2)}) copy-start(f32[64,512]{1,0:T(8,128)S(1)} %fusion.11) | copy-start | bytes 393220
Sparse Core Ops, SparseCore 0:
  47.4 150.5 all-reduce.1
where the time goes:
time: 393 us; the launch traced here: 389 us
  waiting for transfers between devices  151 us (38%)
  other arithmetic  96.6 us (25%)
  matrix products  89.7 us (23%)
  blocking collectives  33.5 us (9%)
  between operations  14.6 us (4%)
  local copies, waits for them, and re-layouts  3.93 us (1%)
    psum x1, waiting for transfers between devices, shards(): gram_full = lax.psum(local_gram, ('wide', 'narrow'))  151 us
    another operation x24, other arithmetic, orthonormal(): lower_factor = jnp.linalg.cholesky(inner)  52.2 us
    another operation x16, other arithmetic, orthonormal(): jax.scipy.linalg.solve_triangular(lower_factor, block.T, lower=True)  44.4 us
    dot_general x1, matrix products, shards(): jnp.dot(unfold, unfold.T, precision=highest, preferred_element_type=jnp.f...  40.1 us
    all_to_all x1, blocking collectives, shards(): lax.all_to_all(core_local, 'wide', split_axis=1, concat_axis=2, tiled=True)  33.5 us
    dot_general x1, matrix products, shards(): jnp.einsum('ir,ijl->lrj', basis, tensor_slab, precision=highest)  25.8 us
    dot_general x8, matrix products, shards(): block = jnp.dot(gram_full, basis, precision=highest)  19 us
  transfers between devices with their start and end apart: 1, of which 1 were waited for; matrix products, arithmetic and copies ran while one was open for 0% of the time, Pallas kernels for 0%

commit v1 on v0

--- a/solution.py
+++ b/solution.py
@@ -17,7 +17,8 @@
     unfold = tensor_slab.reshape(I1, -1)
     basis = start_basis
     local_gram = jnp.dot(unfold, unfold.T, precision=highest, preferred_element_type=jnp.float32)
-    gram_full = lax.psum(local_gram, ("wide", "narrow"))
+    one_axis = lax.psum(local_gram, "wide")
+    gram_full = lax.psum(one_axis, "narrow")
     for sweep_index in range(ITERS):
         block = jnp.dot(gram_full, basis, precision=highest)
         basis = orthonormal(block, jnp.dot(block.T, block, precision=highest))

time: 393 us -> 396 us (level)
  the two profiles are of different devices: /device:TPU:1 before, /device:TPU:24 now
where the time goes in v1:
time: 396 us; the launch traced here: 392 us
  waiting for transfers between devices  151 us (38%)
  other arithmetic  96.6 us (24%)
  matrix products  89.3 us (23%)
  blocking collectives  36.3 us (9%)
  between operations  14.6 us (4%)
    psum x1, waiting for transfers between devices, shards(): one_axis = lax.psum(local_gram, 'wide')  89 us
    psum x1, waiting for transfers between devices, shards(): gram_full = lax.psum(one_axis, 'narrow')  61.6 us
    another operation x24, other arithmetic, orthonormal(): lower_factor = jnp.linalg.cholesky(inner)  52.2 us
    another operation x16, other arithmetic, orthonormal(): jax.scipy.linalg.solve_triangular(lower_factor, block.T, lower=True)  44.4 us
    dot_general x1, matrix products, shards(): jnp.dot(unfold, unfold.T, precision=highest, preferred_element_type=jnp.f...  39.6 us
    all_to_all x1, blocking collectives, shards(): lax.all_to_all(core_local, 'wide', split_axis=1, concat_axis=2, tiled=True)  36.3 us
    dot_general x1, matrix products, shards(): jnp.einsum('ir,ijl->lrj', basis, tensor_slab, precision=highest)  25.8 us
    dot_general x8, matrix products, shards(): block = jnp.dot(gram_full, basis, precision=highest)  19 us
  transfers between devices with their start and end apart: 2, of which 2 were waited for; matrix products, arithmetic and copies ran while one was open for 0% of the time, Pallas kernels for 0%

profile of v1, /device:TPU:24, one launch (start us, length us, event | category | flops | bytes accessed | tf_op | source)
XLA Modules:
  0.0 391.8 jit_solution(14627306743008608503)
XLA Ops:
  7.2 39.6 %fusion.7 = f32[512,512]{1,0:T(8,128)} fusion(f32[512,32,256]{2,1,0:T(8,128)} %param.5), kind=kOutput, calls=%fused_computation.5 | convolution fusion | flops 25769803776 | bytes 17825792 | tf_op jit(solution)/shard_map/dot_general | solution.py:19
  47.4 89.0 %all-reduce.3.cloned.1.call-done = f32[512,512]{1,0:T(8,128)} async-done(((f32[512,512]{1,0:T(8,128)}), f32[512,512]{1,0:T(8,128)}) %all-reduce.3.cloned.1.call-update) | async-done | bytes 1048592 | tf_op jit(solution)/shard_map/psum | solution.py:20
  136.4 61.6 %all-reduce.5.cloned.1.call-done = f32[512,512]{1,0:T(8,128)} async-done(((f32[512,512]{1,0:T(8,128)}), f32[512,512]{1,0:T(8,128)}) %all-reduce.5.cloned.1.call-update) | async-done | bytes 1048592 | tf_op jit(solution)/shard_map/psum | solution.py:21
  197.9 2.4 fusion.65
  200.7 5.8 %cholesky.134 = f32[64,64]{1,0:T(8,128)S(1)} custom-call(f32[64,64]{1,0:T(8,128)S(1)} %fusion.50), custom_call_target="Cholesky" | custom-call | tf_op jit(solution)/shard_map/jit(cholesky)/cholesky | solution.py:11
  207.2 0.7 fusion.27
  207.8 4.9 %custom-call.12 = f32[1,64,64]{1,2,0:T(8,128)S(1)} custom-call(f32[1,64,64]{2,1,0:T(8,128)S(1)} %fusion.27), custom_call_target="InvertDiagBlocksLowerTriangular" | custom-call | tf_op jit(solution)/shard_map/jit(_solve_triangular)/triangular_solve | solution.py:12
  213.1 2.4 fusion.67
  215.8 5.8 %cholesky.145 = f32[64,64]{1,0:T(8,128)S(1)} custom-call(f32[64,64]{1,0:T(8,128)S(1)} %fusion.48), custom_call_target="Cholesky" | custom-call | tf_op jit(solution)/shard_map/jit(cholesky)/cholesky | solution.py:11
  223.0 4.9 %custom-call.13 = f32[1,64,64]{1,2,0:T(8,128)S(1)} custom-call(f32[1,64,64]{2,1,0:T(8,128)S(1)} %fusion.28), custom_call_target="InvertDiagBlocksLowerTriangular" | custom-call | tf_op jit(solution)/shard_map/jit(_solve_triangular)/triangular_solve | solution.py:12
  228.2 2.4 fusion.69
  231.0 5.8 %cholesky.156 = f32[64,64]{1,0:T(8,128)S(1)} custom-call(f32[64,64]{1,0:T(8,128)S(1)} %fusion.46), custom_call_target="Cholesky" | custom-call | tf_op jit(solution)/shard_map/jit(cholesky)/cholesky | solution.py:11
  238.1 4.9 %custom-call.14 = f32[1,64,64]{1,2,0:T(8,128)S(1)} custom-call(f32[1,64,64]{2,1,0:T(8,128)S(1)} %fusion.29), custom_call_target="InvertDiagBlocksLowerTriangular" | custom-call | tf_op jit(solution)/shard_map/jit(_solve_triangular)/triangular_solve | solution.py:12
  243.4 2.4 fusion.71
  246.1 5.8 %cholesky.167 = f32[64,64]{1,0:T(8,128)S(1)} custom-call(f32[64,64]{1,0:T(8,128)S(1)} %fusion.44), custom_call_target="Cholesky" | custom-call | tf_op jit(solution)/shard_map/jit(cholesky)/cholesky | solution.py:11
  253.3 4.9 %custom-call.15 = f32[1,64,64]{1,2,0:T(8,128)S(1)} custom-call(f32[1,64,64]{2,1,0:T(8,128)S(1)} %fusion.30), custom_call_target="InvertDiagBlocksLowerTriangular" | custom-call | tf_op jit(solution)/shard_map/jit(_solve_triangular)/triangular_solve | solution.py:12
  258.5 2.5 fusion.73
  261.4 5.8 %cholesky.178 = f32[64,64]{1,0:T(8,128)S(1)} custom-call(f32[64,64]{1,0:T(8,128)S(1)} %fusion.42), custom_call_target="Cholesky" | custom-call | tf_op jit(solution)/shard_map/jit(cholesky)/cholesky | solution.py:11
  268.6 4.9 %custom-call.16 = f32[1,64,64]{1,2,0:T(8,128)S(1)} custom-call(f32[1,64,64]{2,1,0:T(8,128)S(1)} %fusion.31), custom_call_target="InvertDiagBlocksLowerTriangular" | custom-call | tf_op jit(solution)/shard_map/jit(_solve_triangular)/triangular_solve | solution.py:12
  273.9 2.4 fusion.75
  276.6 5.8 %cholesky.189 = f32[64,64]{1,0:T(8,128)S(1)} custom-call(f32[64,64]{1,0:T(8,128)S(1)} %fusion.40), custom_call_target="Cholesky" | custom-call | tf_op jit(solution)/shard_map/jit(cholesky)/cholesky | solution.py:11
  283.8 4.9 %custom-call.17 = f32[1,64,64]{1,2,0:T(8,128)S(1)} custom-call(f32[1,64,64]{2,1,0:T(8,128)S(1)} %fusion.32), custom_call_target="InvertDiagBlocksLowerTriangular" | custom-call | tf_op jit(solution)/shard_map/jit(_solve_triangular)/triangular_solve | solution.py:12
  289.0 2.4 fusion.77
  291.7 5.8 %cholesky.200 = f32[64,64]{1,0:T(8,128)S(1)} custom-call(f32[64,64]{1,0:T(8,128)S(1)} %fusion.38), custom_call_target="Cholesky" | custom-call | tf_op jit(solution)/shard_map/jit(cholesky)/cholesky | solution.py:11
  298.9 4.9 %custom-call.18 = f32[1,64,64]{1,2,0:T(8,128)S(1)} custom-call(f32[1,64,64]{2,1,0:T(8,128)S(1)} %fusion.33), custom_call_target="InvertDiagBlocksLowerTriangular" | custom-call | tf_op jit(solution)/shard_map/jit(_solve_triangular)/triangular_solve | solution.py:12
  304.1 2.4 fusion.79
  306.9 5.8 %cholesky.211 = f32[64,64]{1,0:T(8,128)S(1)} custom-call(f32[64,64]{1,0:T(8,128)S(1)} %fusion.36), custom_call_target="Cholesky" | custom-call | tf_op jit(solution)/shard_map/jit(cholesky)/cholesky | solution.py:11
  314.0 4.9 %custom-call.19 = f32[1,64,64]{1,2,0:T(8,128)S(1)} custom-call(f32[1,64,64]{2,1,0:T(8,128)S(1)} %fusion.34), custom_call_target="InvertDiagBlocksLowerTriangular" | custom-call | tf_op jit(solution)/shard_map/jit(_solve_triangular)/triangular_solve | solution.py:12
  319.3 25.8 %fusion.4 = f32[256,64,32]{0,1,2:T(8,128)S(1)} fusion(f32[512,32,256]{2,1,0:T(8,128)} %param.5, f32[64,512]{1,0:T(8,128)S(1)} %fusion.11), kind=kOutput, calls=%fused_computation.4 | convolution fusion | flops 3221225472 | bytes 19005440 | tf_op jit(solution)/shard_map/ir,ijl->lrj/dot_general | solution.py:25
  345.1 1.2 copy.53
  346.4 36.3 %all_to_all.18 = f32[256,64,32]{0,2,1:T(8,128)S(1)} all-to-all(f32[256,64,32]{0,2,1:T(8,128)S(1)} %copy.53), channel_id=1, replica_groups=mesh['wide'=16,'narrow'=8] {'wide'}, dimensions={1} | all-to-all | bytes 4194304 | tf_op jit(solution)/shard_map/all_to_all | solution.py:26
  382.8 2.0 copy.55
  (64 shorter events, 16.1 us)
Async XLA Ops:
  7.2 190.8 %copy-start = (f32[512,64]{0,1:T(8,128)S(1)}, f32[512,64]{0,1:T(8,128)}, u32[]{:S(2)}) copy-start(f32[512,64]{0,1:T(8,128)} %param.6) | copy-start | bytes 393220
  7.2 129.2 %all-reduce.3.cloned.1.call-start = ((), (), s32[]{:S(2)}) async-start(), calls=%async_computation.1 | async-start | bytes 2097152 | tf_op jit(solution)/shard_map/psum | solution.py:20
  46.9 151.1 %all-reduce.5.cloned.1.call-start = ((), (), s32[]{:S(2)}) async-start(), calls=%async_computation.2 | async-start | bytes 2097152 | tf_op jit(solution)/shard_map/psum | solution.py:21
  319.3 65.4 %copy-start.1 = (f32[64,512]{1,0:T(8,128)}, f32[64,512]{1,0:T(8,128)S(1)}, u32[]{:S(2)}) copy-start(f32[64,512]{1,0:T(8,128)S(1)} %fusion.11) | copy-start | bytes 393220
Sparse Core Ops, SparseCore 0:
  47.0 89.3 all-reduce.2
  138.7 59.2 all-reduce.4
